TPU v7x, 32 devices: a whole 2x2x4 slice. The times are simulated.
32 devices in a mesh: lon: 8 (over z, y), lat: 2 (over core), mem: 2 (over x).
Axes of the slice: x: 2, y: 2, z: 4, core: 2. Of those that a mesh axis runs over, the one named last changes fastest.
Arguments:
- inputs: bfloat16 [2, 48, 896, 512], P('mem', 'lat', 'lon'), may hold values from -6 to 6
- cotangent: bfloat16 [2, 48, 896, 512], P('mem', 'lat', 'lon'), may hold values from -6 to 6
- dw_kernel: bfloat16 [2, 9, 512], replicated, may hold values from -4 to 4
- pw_weight: bfloat16 [2, 512, 512], replicated, may hold values from -0.25 to 0.25
Outputs:
- input_grad: bfloat16 [2, 48, 896, 512], P('mem', 'lat', 'lon')
- kernel_grad: float32 [2, 9, 512], P(None, None, 'mem')
- weight_grad: float32 [2, 512, 512], P(None, None, 'mem')
All inputs are finite; a program needn't handle non-finite values.
Results may differ from a plain program's by a relative error of at most 0.015.
Values may be sent and summed in bfloat16 or wider, within the bound.
A program may use at most 128 MiB of HBM per device.

v0:
```python
import functools
import math

import jax
import jax.numpy as jnp
from jax import lax
from jax.experimental import pallas as pl
from jax.experimental.pallas import tpu as pltpu
from jax.sharding import PartitionSpec as P

S = 4
F32 = jnp.float32
BF16 = jnp.bfloat16
MESH = pl.DeviceIdType.MESH
ROOT = math.sqrt(2.0 / math.pi)
CUBE = 0.044715


def gelu(x):
    return 0.5 * x * (1.0 + jnp.tanh(ROOT * (x + CUBE * (x * x * x))))


def gelu_slope(x):
    xx = x * x
    t = jnp.tanh(ROOT * (x + CUBE * (x * xx)))
    return 0.5 * (1.0 + t) + (0.5 * ROOT) * x * (1.0 - t * t) * (1.0 + (3.0 * CUBE) * xx)


def kernel(
    n, factor,
    x_hbm, cot_hbm, dw_ref, w_ref,
    out_hbm, kgrad, wgrad,
    raw, cotraw, u0p, u1p, g1p, g0p, g1, hid0, hid1, gp, d0, rc0, rc1, pre,
    perm, unperm, kb, kacc, wacc,
    w0s, w0r, w1s, w1r, w2s, w2r, w3s, w3r, kv, kr0, ks1, kr1, ks2, kr2,
    in_sem, out_sem, rim_s, rim_r, red_s, red_r,
):
    R, A, T, C = hid0.shape
    M = A * T
    H = C // 2
    ch = max(c for c in (1, 2, 4) if A % c == 0)
    groups = [slice(g, g + 128) for g in range(0, C, 128)]
    me, lat, mem = lax.axis_index("lon"), lax.axis_index("lat"), lax.axis_index("mem")
    other, omem = 1 - lat, 1 - mem

    def lon_at(d):
        return lax.rem(me + (d % n), n)

    def dev(lon_i, lat_i, mem_i):
        return {"lon": lon_i, "lat": lat_i, "mem": mem_i}

    def remote(src, dst, ssem, rsem, where):
        c = pltpu.make_async_remote_copy(
            src_ref=src, dst_ref=dst, send_sem=ssem, recv_sem=rsem, device_id=where, device_id_type=MESH
        )
        c.start()
        return c

    in_copies = []
    for i, (src, dst) in enumerate(((x_hbm, raw), (cot_hbm, cotraw))):
        for r in range(R):
            c = pltpu.make_async_copy(src.at[0, pl.ds(S * r, S)], dst.at[pl.ds(S * r, S)], in_sem.at[i, r])
            c.start()
            in_copies.append(c)

    barrier = pltpu.get_barrier_semaphore()
    for d in range(n):
        for la in (lat, other):
            if d == 0 and la is lat:
                continue
            pl.semaphore_signal(barrier, inc=1, device_id=dev(lon_at(d), la, mem), device_id_type=MESH)
    pl.semaphore_signal(barrier, inc=1, device_id=dev(me, lat, omem), device_id_type=MESH)

    def one_hot(rows_dim):
        o = lax.broadcasted_iota(jnp.int32, (M, M), rows_dim)
        i = lax.broadcasted_iota(jnp.int32, (M, M), 1 - rows_dim)
        a, s, b = o >> 4, (o >> 2) & 3, o & 3
        return jnp.where(i == s * (A * S) + a * S + b, 1.0, 0.0).astype(BF16)

    perm[...] = one_hot(0)
    unperm[...] = one_hot(1)
    for l in range(2):
        taps_f = dw_ref[l].astype(F32)
        for t in range(9):
            kb[l, t] = jnp.broadcast_to(taps_f[t : t + 1, :], (8, C))
    kacc[...] = jnp.zeros_like(kacc)
    kv[...] = jnp.zeros_like(kv)
    edge = lat * (R + 1)
    for ref in (u0p, u1p, g1p, g0p):
        ref[edge] = jnp.zeros(ref.shape[1:], BF16)

    def regroup(src, r):
        rows = src[pl.ds(S * r, S)].reshape(M, C)
        return jnp.dot(perm[...], rows, preferred_element_type=F32).astype(BF16).reshape(A, T, C)

    for r in range(R):
        in_copies[r].wait()
        u0p[1 + r, 1 : A + 1] = regroup(raw, r)

    pl.semaphore_wait(barrier, 2 * n)

    def rims(ref, e):
        right, left = lon_at(1), lon_at(-1)
        row = R - lat * (R - 1)
        moves = (
            (ref.at[pl.ds(1, R), pl.ds(A, 1)], ref.at[pl.ds(1, R), pl.ds(0, 1)], dev(right, lat, mem)),
            (ref.at[pl.ds(1, R), pl.ds(1, 1)], ref.at[pl.ds(1, R), pl.ds(A + 1, 1)], dev(left, lat, mem)),
            (ref.at[row, pl.ds(1, A)], ref.at[edge, pl.ds(1, A)], dev(me, other, mem)),
            (ref.at[row, pl.ds(A, 1)], ref.at[edge, pl.ds(0, 1)], dev(right, other, mem)),
            (ref.at[row, pl.ds(1, 1)], ref.at[edge, pl.ds(A + 1, 1)], dev(left, other, mem)),
        )
        return [remote(s, d, rim_s.at[e, i], rim_r.at[e, i], w) for i, (s, d, w) in enumerate(moves)]

    def finish(copies):
        for c in copies:
            c.wait()

    def wide(v):
        return v.astype(F32).reshape(2 * ch, 8, 128)

    def tap(ref, r, a, t, lanes, rev):
        p, q = divmod(t, 3)
        if rev:
            p, q = 2 - p, 2 - q
        return wide(ref[r + p, pl.ds(a + q, ch), :, lanes])

    def chunks(fn):
        def step(i, c):
            fn(i * ch)
            return c

        lax.fori_loop(0, A // ch, step, 0)

    def rows_loop(lo, hi, fn):
        def step(r, c):
            fn(r)
            return c

        lax.fori_loop(lo, hi, step, 0)

    def conv_norm(src, l, r, hid, rc, rr):
        def go(a):
            convs = []
            for lanes in groups:
                acc = tap(src, r, a, 0, lanes, False) * kb[l, 0, :, lanes]
                for t in range(1, 9):
                    acc = acc + tap(src, r, a, t, lanes, False) * kb[l, t, :, lanes]
                convs.append(acc)
            sq = sum(c * c for c in convs)
            recip = lax.rsqrt(jnp.sum(sq, axis=-1, keepdims=True) * (1.0 / C) + 1e-6)
            recip = jnp.broadcast_to(recip, (2 * ch, 8, 128))
            rc[rr, pl.ds(a, ch)] = recip.reshape(ch, T, 128)
            for lanes, c in zip(groups, convs):
                hid[r, pl.ds(a, ch), :, lanes] = (c * recip).reshape(ch, T, 128).astype(BF16)

        chunks(go)

    def mix(v, l):
        return jnp.dot(v.reshape(M, C), w_ref[l], preferred_element_type=F32).reshape(A, T, C)

    def mix_back(v, l):
        return lax.dot_general(
            v.reshape(M, C), w_ref[l], (((1,), (1,)), ((), ())), preferred_element_type=F32
        ).reshape(A, T, C)

    def norm_back(dst, hid, rc, r, rr):
        def go(a):
            ns = [wide(hid[r, pl.ds(a, ch), :, lanes]) for lanes in groups]
            gs = [pre[pl.ds(a, ch), :, lanes].reshape(2 * ch, 8, 128) for lanes in groups]
            dots = sum(g * v for g, v in zip(gs, ns))
            mean = jnp.sum(dots, axis=-1, keepdims=True) * (1.0 / C)
            recip = rc[rr, pl.ds(a, ch)].reshape(2 * ch, 8, 128)
            for lanes, g, v in zip(groups, gs, ns):
                dst[1 + r, pl.ds(1 + a, ch), :, lanes] = (recip * (g - v * mean)).reshape(ch, T, 128).astype(BF16)

        chunks(go)

    def weight_sum(l, hid):
        wacc[l] = jnp.zeros((C, C), F32)

        def go(r):
            wacc[l] += lax.dot_general(
                hid[r].reshape(M, C), gp[r].reshape(M, C), (((0,), (0,)), ((), ())), preferred_element_type=F32
            )

        rows_loop(0, R, go)

    own_rows = pl.ds(pl.multiple_of(lat * H, H), H)
    other_rows = pl.ds(pl.multiple_of(other * H, H), H)
    own_cols = pl.ds(pl.multiple_of(mem * H, H), H)
    other_cols = pl.ds(pl.multiple_of(omem * H, H), H)
    piece = H // n
    wire = w2s.dtype

    def red(l, stage, i, src, dst, where):
        return remote(src, dst, red_s.at[l, stage, i], red_r.at[l, stage, i], where)

    def stage0(l):
        w0s[l] = wacc[l, other_rows, :].astype(BF16)
        out = [red(l, 0, 0, w0s.at[l], w0r.at[l], dev(me, other, mem))]
        if l == 0:
            for k in range(2):
                for t in range(9):
                    kv[k, t : t + 1, :] = jnp.sum(kacc[k, t], axis=0, keepdims=True)
            out.append(red(l, 0, 1, kv, kr0, dev(me, other, mem)))
        return out

    def stage1(l):
        wacc[l, own_rows, :] += w0r[l].astype(F32)
        w1s[l] = wacc[l, own_rows, other_cols].astype(BF16)
        out = [red(l, 1, 0, w1s.at[l], w1r.at[l], dev(me, lat, omem))]
        if l == 0:
            kv[...] += kr0[...]
            ks1[...] = kv[:, :, other_cols]
            out.append(red(l, 1, 1, ks1, kr1, dev(me, lat, omem)))
        return out

    def stage2(l):
        total = wacc[l, own_rows, own_cols] + w1r[l].astype(F32)
        wacc[l, own_rows, own_cols] = total
        w2s[l] = total.reshape(n, piece, H).astype(wire)
        out = []
        if l == 0:
            both = kv[:, :, own_cols] + kr1[...]
            ks2[...] = both
            kr2[me] = both
        for d in range(1, n):
            to = lon_at(d)
            out.append(red(l, 2, d, w2s.at[l, to], w2r.at[l, me], dev(to, lat, mem)))
            if l == 0:
                out.append(red(l, 2, n + d, ks2, kr2.at[me], dev(to, lat, mem)))
        return out

    def stage3(l):
        start = pl.multiple_of(lat * H + me * piece, piece)
        total = wacc[l, pl.ds(start, piece), own_cols]
        for d in range(1, n):
            total = total + w2r[l, lon_at(d)].astype(F32)
        done = (total * factor).astype(wire)
        w3s[l] = done
        w3r[l, lat, me] = done
        out = []
        for d in range(n):
            for k, la in enumerate((lat, other)):
                if d or k:
                    out.append(red(l, 3, k * n + d, w3s.at[l], w3r.at[l, lat, me], dev(lon_at(d), la, mem)))
        if l == 0:
            ks = kr2[0]
            for j in range(1, n):
                ks = ks + kr2[j]
            for k in range(2):
                kgrad[k] = ks[k, :9, :] * factor
        return out

    def stage4(l):
        wgrad[l] = w3r[l].reshape(C, H).astype(F32)

    moving = rims(u0p, 0)
    for r in range(R):
        in_copies[R + r].wait()
        g1[r] = regroup(cotraw, r)
    finish(moving)

    def block0(r):
        conv_norm(u0p, 0, r, hid0, rc0, r)
        d0[r] = mix(hid0[r], 0)

        def go(a):
            for lanes in groups:
                x = d0[r, pl.ds(a, ch), :, lanes]
                u = u0p[1 + r, pl.ds(1 + a, ch), :, lanes].astype(F32)
                u1p[1 + r, pl.ds(1 + a, ch), :, lanes] = (u + gelu(x)).astype(BF16)

        chunks(go)

    rows_loop(0, R, block0)
    moving = rims(u1p, 1)

    def slopes(r):
        def go(a):
            for lanes in groups:
                d0[r, pl.ds(a, ch), :, lanes] = gelu_slope(d0[r, pl.ds(a, ch), :, lanes])

        chunks(go)

    rows_loop(0, R, slopes)
    finish(moving)

    def block1(r):
        conv_norm(u1p, 1, r, hid1, rc1, 0)
        pre[...] = mix(hid1[r], 1)

        def go(a):
            for lanes in groups:
                g = g1[r, pl.ds(a, ch), :, lanes].astype(F32)
                gp[r, pl.ds(a, ch), :, lanes] = (g * gelu_slope(pre[pl.ds(a, ch), :, lanes])).astype(BF16)

        chunks(go)
        pre[...] = mix_back(gp[r], 1)
        norm_back(g1p, hid1, rc1, r, 0)

    rows_loop(0, R, block1)
    moving = rims(g1p, 2)
    weight_sum(1, hid1)
    sums = stage0(1)
    finish(moving)

    def back0(r):
        def go(a):
            for lanes in groups:
                s = wide(g1[r, pl.ds(a, ch), :, lanes])
                u = wide(u1p[1 + r, pl.ds(1 + a, ch), :, lanes])
                for t in range(9):
                    v = tap(g1p, r, a, t, lanes, True)
                    s = s + v * kb[1, t, :, lanes]
                    kacc[1, t, :, lanes] += jnp.sum(v * u, axis=0)
                g = s.reshape(ch, T, 128).astype(BF16)
                g1[r, pl.ds(a, ch), :, lanes] = g
                gp[r, pl.ds(a, ch), :, lanes] = (g.astype(F32) * d0[r, pl.ds(a, ch), :, lanes]).astype(BF16)

        chunks(go)
        pre[...] = mix_back(gp[r], 0)
        norm_back(g0p, hid0, rc0, r, r)

    cuts = [(R * i) // 3 for i in range(4)]
    for i, stage in enumerate((stage1, stage2, stage3)):
        rows_loop(cuts[i], cuts[i + 1], back0)
        finish(sums)
        sums = stage(1)
    moving = rims(g0p, 3)
    weight_sum(0, hid0)

    def taps0(r):
        def go(a):
            for lanes in groups:
                g = wide(g0p[1 + r, pl.ds(1 + a, ch), :, lanes])
                for t in range(9):
                    kacc[0, t, :, lanes] += jnp.sum(tap(u0p, r, a, t, lanes, False) * g, axis=0)

        chunks(go)

    rows_loop(0, R, taps0)
    finish(sums)
    stage4(1)
    sums = stage0(0)
    finish(moving)

    def last(r):
        def go(a):
            for lanes in groups:
                s = wide(g1[r, pl.ds(a, ch), :, lanes])
                for t in range(9):
                    s = s + tap(g0p, r, a, t, lanes, True) * kb[0, t, :, lanes]
                hid1[r, pl.ds(a, ch), :, lanes] = s.reshape(ch, T, 128).astype(BF16)

        chunks(go)
        rows = jnp.dot(unperm[...], hid1[r].reshape(M, C), preferred_element_type=F32).astype(BF16)
        raw[pl.ds(S * r, S)] = rows.reshape(S, S * A, C)

    out_copies = []
    for i, stage in enumerate((stage1, stage2, stage3)):
        rows_loop(cuts[i], cuts[i + 1], last)
        for r in range(cuts[i], cuts[i + 1]):
            c = pltpu.make_async_copy(raw.at[pl.ds(S * r, S)], out_hbm.at[0, pl.ds(S * r, S)], out_sem.at[r])
            c.start()
            out_copies.append(c)
        finish(sums)
        sums = stage(0)
    finish(sums)
    stage4(0)
    finish(out_copies)


def body(inputs, cotangent, dw_kernel, pw_weight):
    _, rows, cols, C = inputs.shape
    n = lax.axis_size("lon")
    R, A, T, H = rows // S, cols // S, S * S, C // 2
    piece = H // n
    wire = BF16 if piece % 16 == 0 else F32
    samples = inputs.size // C * n * lax.axis_size("lat") * lax.axis_size("mem")
    anywhere = pl.BlockSpec(memory_space=pl.ANY)
    local = pl.BlockSpec(memory_space=pltpu.VMEM)
    padded = pltpu.VMEM((R + 2, A + 2, T, C), BF16)
    cells = pltpu.VMEM((R, A, T, C), BF16)
    scratch = [
        pltpu.VMEM((rows, cols, C), BF16),
        pltpu.VMEM((rows, cols, C), BF16),
        padded, padded, padded, padded,
        cells, cells, cells, cells,
        pltpu.VMEM((R, A, T, C), F32),
        pltpu.VMEM((R, A, T, 128), F32),
        pltpu.VMEM((1, A, T, 128), F32),
        pltpu.VMEM((A, T, C), F32),
        pltpu.VMEM((A * T, A * T), BF16),
        pltpu.VMEM((A * T, A * T), BF16),
        pltpu.VMEM((2, 9, 8, C), F32),
        pltpu.VMEM((2, 9, 8, C), F32),
        pltpu.VMEM((2, C, C), F32),
        pltpu.VMEM((2, H, C), BF16), pltpu.VMEM((2, H, C), BF16),
        pltpu.VMEM((2, H, H), BF16), pltpu.VMEM((2, H, H), BF16),
        pltpu.VMEM((2, n, piece, H), wire), pltpu.VMEM((2, n, piece, H), wire),
        pltpu.VMEM((2, piece, H), wire), pltpu.VMEM((2, 2, n, piece, H), wire),
        pltpu.VMEM((2, 16, C), F32), pltpu.VMEM((2, 16, C), F32),
        pltpu.VMEM((2, 16, H), F32), pltpu.VMEM((2, 16, H), F32),
        pltpu.VMEM((2, 16, H), F32), pltpu.VMEM((n, 2, 16, H), F32),
        pltpu.SemaphoreType.DMA((2, R)), pltpu.SemaphoreType.DMA((R,)),
        pltpu.SemaphoreType.DMA((4, 5)), pltpu.SemaphoreType.DMA((4, 5)),
        pltpu.SemaphoreType.DMA((2, 4, 2 * n)), pltpu.SemaphoreType.DMA((2, 4, 2 * n)),
    ]
    return pl.pallas_call(
        functools.partial(kernel, n, 1.0 / math.sqrt(samples)),
        out_shape=(
            jax.ShapeDtypeStruct(inputs.shape, BF16),
            jax.ShapeDtypeStruct((2, 9, H), F32),
            jax.ShapeDtypeStruct((2, C, H), F32),
        ),
        in_specs=[anywhere, anywhere, local, local],
        out_specs=(anywhere, local, local),
        scratch_shapes=scratch,
        name="blocks",
        compiler_params=pltpu.CompilerParams(
            collective_id=0, has_side_effects=True, vmem_limit_bytes=60 * 1024 * 1024
        ),
    )(inputs, cotangent, dw_kernel, pw_weight)


def solution(mesh):
    placed = (P("mem", "lat", "lon", None), P("mem", "lat", "lon", None), P(), P())
    return jax.shard_map(
        body,
        mesh=mesh,
        in_specs=placed,
        out_specs=(P("mem", "lat", "lon", None), P(None, None, "mem"), P(None, None, "mem")),
        check_vma=False,
    )
```

profile of v0, /device:TPU:0, one launch (start us, length us, event | category | flops | bytes accessed | tf_op | source)
XLA Modules:
  0.0 126.1 jit_solution(2418593505911640839)
XLA Ops:
  0.6 1.3 %copy.7.dw_ref = bf16[2,9,512]{2,1,0:T(8,128)(2,1)} copy(bf16[2,9,512]{2,0,1:T(2,128)(2,1)} %param.6) | data formatting | bytes 36864 | tf_op args[2]
  2.0 118.2 %blocks.1 = (bf16[1,24,112,512]{3,2,1,0:T(8,128)(2,1)}, f32[2,9,256]{2,1,0:T(8,128)}, f32[2,512,256]{2,1,0:T(8,128)}) custom-call(bf16[1,24,112,512]{3,2,1,0:T(8,128)(2,1)} %x_hbm.1, bf16[1,24,112,512]{3,2,1,0:T(8,128)(2,1)} %cot_hbm.1, bf16[2,9,512]{2,1,0:T(8,128)(2,1)} %copy.7.dw_ref, bf16[2,512,512]{2,1,0:T(8,128)(2,1)} %w_ref.1), custom_call_target="tpu_custom_call" | custom-call | tf_op jit(solution)/shard_map/blocks/pallas_call | solution.py:410
  120.2 1.4 %copy.8 = f32[2,9,256]{2,0,1:T(2,128)} copy(f32[2,9,256]{2,1,0:T(8,128)} %get-tuple-element.4) | data formatting | bytes 36864 | tf_op jit(solution)/shard_map/blocks/pallas_call | solution.py:410
  121.6 0.0 copy-start
  121.6 3.6 %copy.11 = bf16[1,24,112,512]{3,2,1,0:T(8,128)(2,1)} copy(bf16[1,24,112,512]{3,2,1,0:T(8,128)(2,1)} %get-tuple-element.9) | data formatting | bytes 5505024
  125.2 0.0 copy-done
  125.2 1.0 copy.12
Async XLA Ops:
  121.6 3.6 %copy-start = (f32[2,512,256]{2,1,0:T(8,128)S(1)}, f32[2,512,256]{2,1,0:T(8,128)}, u32[]{:S(2)}) copy-start(f32[2,512,256]{2,1,0:T(8,128)} %get-tuple-element.11) | copy-start | bytes 3145732
where the time goes:
time: 126 us
  Pallas kernels  118 us (94%)
  local copies, waits for them, and re-layouts  7.29 us (6%)
    pallas_call x1, Pallas kernels, body(): pl.pallas_call(functools.partial(kernel, n, 1.0 / math.sqrt(samples)), ou...  118 us
    unnamed x5, local copies, waits for them, and re-layouts  5.91 us

commit v1 on v0

--- a/solution.py
+++ b/solution.py
@@ -118,11 +118,12 @@
     def wide(v):
         return v.astype(F32).reshape(2 * ch, 8, 128)
 
-    def tap(ref, r, a, t, lanes, rev):
-        p, q = divmod(t, 3)
-        if rev:
-            p, q = 2 - p, 2 - q
-        return wide(ref[r + p, pl.ds(a + q, ch), :, lanes])
+    def taps(ref, r, a, lanes, rev):
+        for p in range(3):
+            row = ref[r + p, pl.ds(a, ch + 2), :, lanes].astype(F32).reshape(2 * ch + 4, 8, 128)
+            for q in range(3):
+                t = 3 * (2 - p) + 2 - q if rev else 3 * p + q
+                yield t, row[2 * q : 2 * q + 2 * ch]
 
     def chunks(fn):
         def step(i, c):
@@ -142,9 +143,9 @@
         def go(a):
             convs = []
             for lanes in groups:
-                acc = tap(src, r, a, 0, lanes, False) * kb[l, 0, :, lanes]
-                for t in range(1, 9):
-                    acc = acc + tap(src, r, a, t, lanes, False) * kb[l, t, :, lanes]
+                acc = 0.0
+                for t, v in taps(src, r, a, lanes, False):
+                    acc = acc + v * kb[l, t, :, lanes]
                 convs.append(acc)
             sq = sum(c * c for c in convs)
             recip = lax.rsqrt(jnp.sum(sq, axis=-1, keepdims=True) * (1.0 / C) + 1e-6)
@@ -197,39 +198,45 @@
 
     def stage0(l):
         w0s[l] = wacc[l, other_rows, :].astype(BF16)
-        out = [red(l, 0, 0, w0s.at[l], w0r.at[l], dev(me, other, mem))]
-        if l == 0:
-            for k in range(2):
-                for t in range(9):
-                    kv[k, t : t + 1, :] = jnp.sum(kacc[k, t], axis=0, keepdims=True)
-            out.append(red(l, 0, 1, kv, kr0, dev(me, other, mem)))
-        return out
+        return [red(l, 0, 0, w0s.at[l], w0r.at[l], dev(me, other, mem))]
+
+    def taps_stage0():
+        for k in range(2):
+            for t in range(9):
+                kv[k, t : t + 1, :] = jnp.sum(kacc[k, t], axis=0, keepdims=True)
+        return [red(0, 0, 1, kv, kr0, dev(me, other, mem))]
+
+    def taps_stage1():
+        kv[...] += kr0[...]
+        ks1[...] = kv[:, :, other_cols]
+        return [red(0, 1, 1, ks1, kr1, dev(me, lat, omem))]
+
+    def taps_stage2():
+        both = (kv[:, :, own_cols] + kr1[...]).astype(BF16)
+        ks2[...] = both
+        kr2[me] = both
+        return [red(0, 2, n + d, ks2, kr2.at[me], dev(lon_at(d), lat, mem)) for d in range(1, n)]
+
+    def taps_stage3():
+        ks = kr2[0].astype(F32)
+        for j in range(1, n):
+            ks = ks + kr2[j].astype(F32)
+        for k in range(2):
+            kgrad[k] = ks[k, :9, :] * factor
+        return []
 
     def stage1(l):
         wacc[l, own_rows, :] += w0r[l].astype(F32)
         w1s[l] = wacc[l, own_rows, other_cols].astype(BF16)
-        out = [red(l, 1, 0, w1s.at[l], w1r.at[l], dev(me, lat, omem))]
-        if l == 0:
-            kv[...] += kr0[...]
-            ks1[...] = kv[:, :, other_cols]
-            out.append(red(l, 1, 1, ks1, kr1, dev(me, lat, omem)))
-        return out
+        return [red(l, 1, 0, w1s.at[l], w1r.at[l], dev(me, lat, omem))]
 
     def stage2(l):
         total = wacc[l, own_rows, own_cols] + w1r[l].astype(F32)
         wacc[l, own_rows, own_cols] = total
         w2s[l] = total.reshape(n, piece, H).astype(wire)
-        out = []
-        if l == 0:
-            both = kv[:, :, own_cols] + kr1[...]
-            ks2[...] = both
-            kr2[me] = both
-        for d in range(1, n):
-            to = lon_at(d)
-            out.append(red(l, 2, d, w2s.at[l, to], w2r.at[l, me], dev(to, lat, mem)))
-            if l == 0:
-                out.append(red(l, 2, n + d, ks2, kr2.at[me], dev(to, lat, mem)))
-        return out
+        return [
+            red(l, 2, d, w2s.at[l, lon_at(d)], w2r.at[l, me], dev(lon_at(d), lat, mem)) for d in range(1, n)
+        ]
 
     def stage3(l):
         start = pl.multiple_of(lat * H + me * piece, piece)
@@ -244,12 +251,6 @@
             for k, la in enumerate((lat, other)):
                 if d or k:
                     out.append(red(l, 3, k * n + d, w3s.at[l], w3r.at[l, lat, me], dev(lon_at(d), la, mem)))
-        if l == 0:
-            ks = kr2[0]
-            for j in range(1, n):
-                ks = ks + kr2[j]
-            for k in range(2):
-                kgrad[k] = ks[k, :9, :] * factor
         return out
 
     def stage4(l):
@@ -310,8 +311,7 @@
             for lanes in groups:
                 s = wide(g1[r, pl.ds(a, ch), :, lanes])
                 u = wide(u1p[1 + r, pl.ds(1 + a, ch), :, lanes])
-                for t in range(9):
-                    v = tap(g1p, r, a, t, lanes, True)
+                for t, v in taps(g1p, r, a, lanes, True):
                     s = s + v * kb[1, t, :, lanes]
                     kacc[1, t, :, lanes] += jnp.sum(v * u, axis=0)
                 g = s.reshape(ch, T, 128).astype(BF16)
@@ -329,28 +329,31 @@
         sums = stage(1)
     moving = rims(g0p, 3)
     weight_sum(0, hid0)
+    finish(sums)
+    sums = stage0(0)
 
     def taps0(r):
         def go(a):
             for lanes in groups:
                 g = wide(g0p[1 + r, pl.ds(1 + a, ch), :, lanes])
-                for t in range(9):
-                    kacc[0, t, :, lanes] += jnp.sum(tap(u0p, r, a, t, lanes, False) * g, axis=0)
+                for t, v in taps(u0p, r, a, lanes, False):
+                    kacc[0, t, :, lanes] += jnp.sum(v * g, axis=0)
 
         chunks(go)
 
     rows_loop(0, R, taps0)
+    tap_sums = taps_stage0()
     finish(sums)
+    sums = stage1(0)
     stage4(1)
-    sums = stage0(0)
     finish(moving)
 
     def last(r):
         def go(a):
             for lanes in groups:
                 s = wide(g1[r, pl.ds(a, ch), :, lanes])
-                for t in range(9):
-                    s = s + tap(g0p, r, a, t, lanes, True) * kb[0, t, :, lanes]
+                for t, v in taps(g0p, r, a, lanes, True):
+                    s = s + v * kb[0, t, :, lanes]
                 hid1[r, pl.ds(a, ch), :, lanes] = s.reshape(ch, T, 128).astype(BF16)
 
         chunks(go)
@@ -358,15 +361,17 @@
         raw[pl.ds(S * r, S)] = rows.reshape(S, S * A, C)
 
     out_copies = []
-    for i, stage in enumerate((stage1, stage2, stage3)):
+    tap_stages = (taps_stage1, taps_stage2, taps_stage3)
+    for i, stage in enumerate((stage2, stage3, None)):
         rows_loop(cuts[i], cuts[i + 1], last)
         for r in range(cuts[i], cuts[i + 1]):
             c = pltpu.make_async_copy(raw.at[pl.ds(S * r, S)], out_hbm.at[0, pl.ds(S * r, S)], out_sem.at[r])
             c.start()
             out_copies.append(c)
         finish(sums)
-        sums = stage(0)
-    finish(sums)
+        sums = stage(0) if stage else []
+        finish(tap_sums)
+        tap_sums = tap_stages[i]()
     stage4(0)
     finish(out_copies)
 
@@ -402,7 +407,7 @@
         pltpu.VMEM((2, piece, H), wire), pltpu.VMEM((2, 2, n, piece, H), wire),
         pltpu.VMEM((2, 16, C), F32), pltpu.VMEM((2, 16, C), F32),
         pltpu.VMEM((2, 16, H), F32), pltpu.VMEM((2, 16, H), F32),
-        pltpu.VMEM((2, 16, H), F32), pltpu.VMEM((n, 2, 16, H), F32),
+        pltpu.VMEM((2, 16, H), BF16), pltpu.VMEM((n, 2, 16, H), BF16),
         pltpu.SemaphoreType.DMA((2, R)), pltpu.SemaphoreType.DMA((R,)),
         pltpu.SemaphoreType.DMA((4, 5)), pltpu.SemaphoreType.DMA((4, 5)),
         pltpu.SemaphoreType.DMA((2, 4, 2 * n)), pltpu.SemaphoreType.DMA((2, 4, 2 * n)),

time: 126 us -> 124 us (0.984)
  Pallas kernels: 118 us -> 116 us
    pallas_call x1, Pallas kernels: 118 us -> 116 us  [body(): pl.pallas_call(functools.partial(kernel, n, 1.0 / math.sqrt(samples)), ou...]
where the time goes in v1:
time: 124 us
  Pallas kernels  116 us (94%)
  local copies, waits for them, and re-layouts  7.29 us (6%)
    pallas_call x1, Pallas kernels, body(): pl.pallas_call(functools.partial(kernel, n, 1.0 / math.sqrt(samples)), ou...  116 us
    unnamed x5, local copies, waits for them, and re-layouts  5.91 us

profile of v1, /device:TPU:0, one launch (start us, length us, event | category | flops | bytes accessed | tf_op | source)
XLA Modules:
  0.0 123.6 jit_solution(7970101541450311686)
XLA Ops:
  0.6 1.3 %copy.7.dw_ref = bf16[2,9,512]{2,1,0:T(8,128)(2,1)} copy(bf16[2,9,512]{2,0,1:T(2,128)(2,1)} %param.6) | data formatting | bytes 36864 | tf_op args[2]
  2.0 115.6 %blocks.1 = (bf16[1,24,112,512]{3,2,1,0:T(8,128)(2,1)}, f32[2,9,256]{2,1,0:T(8,128)}, f32[2,512,256]{2,1,0:T(8,128)}) custom-call(bf16[1,24,112,512]{3,2,1,0:T(8,128)(2,1)} %x_hbm.1, bf16[1,24,112,512]{3,2,1,0:T(8,128)(2,1)} %cot_hbm.1, bf16[2,9,512]{2,1,0:T(8,128)(2,1)} %copy.7.dw_ref, bf16[2,512,512]{2,1,0:T(8,128)(2,1)} %w_ref.1), custom_call_target="tpu_custom_call" | custom-call | tf_op jit(solution)/shard_map/blocks/pallas_call | solution.py:415
  117.6 1.4 %copy.8 = f32[2,9,256]{2,0,1:T(2,128)} copy(f32[2,9,256]{2,1,0:T(8,128)} %get-tuple-element.4) | data formatting | bytes 36864 | tf_op jit(solution)/shard_map/blocks/pallas_call | solution.py:415
  119.0 0.0 copy-start
  119.0 3.6 %copy.11 = bf16[1,24,112,512]{3,2,1,0:T(8,128)(2,1)} copy(bf16[1,24,112,512]{3,2,1,0:T(8,128)(2,1)} %get-tuple-element.9) | data formatting | bytes 5505024
  122.6 0.0 copy-done
  122.6 1.0 copy.12
Async XLA Ops:
  119.0 3.6 %copy-start = (f32[2,512,256]{2,1,0:T(8,128)S(1)}, f32[2,512,256]{2,1,0:T(8,128)}, u32[]{:S(2)}) copy-start(f32[2,512,256]{2,1,0:T(8,128)} %get-tuple-element.11) | copy-start | bytes 3145732

commit v2 on v1

--- a/solution.py
+++ b/solution.py
@@ -99,17 +99,31 @@
 
     pl.semaphore_wait(barrier, 2 * n)
 
-    def rims(ref, e):
-        right, left = lon_at(1), lon_at(-1)
-        row = R - lat * (R - 1)
+    right, left = lon_at(1), lon_at(-1)
+
+    def send_rims(e, first, moves):
+        return [
+            remote(s, d, rim_s.at[e, i + first], rim_r.at[e, i + first], w) for i, (s, d, w) in enumerate(moves)
+        ]
+
+    def lon_rims(ref, e):
         moves = (
             (ref.at[pl.ds(1, R), pl.ds(A, 1)], ref.at[pl.ds(1, R), pl.ds(0, 1)], dev(right, lat, mem)),
             (ref.at[pl.ds(1, R), pl.ds(1, 1)], ref.at[pl.ds(1, R), pl.ds(A + 1, 1)], dev(left, lat, mem)),
+        )
+        return send_rims(e, 0, moves)
+
+    def lat_rims(ref, e):
+        row = R - lat * (R - 1)
+        moves = (
             (ref.at[row, pl.ds(1, A)], ref.at[edge, pl.ds(1, A)], dev(me, other, mem)),
             (ref.at[row, pl.ds(A, 1)], ref.at[edge, pl.ds(0, 1)], dev(right, other, mem)),
             (ref.at[row, pl.ds(1, 1)], ref.at[edge, pl.ds(A + 1, 1)], dev(left, other, mem)),
         )
-        return [remote(s, d, rim_s.at[e, i], rim_r.at[e, i], w) for i, (s, d, w) in enumerate(moves)]
+        return send_rims(e, 2, moves)
+
+    def inward(i):
+        return i + other * (R - 1 - 2 * i)
 
     def finish(copies):
         for c in copies:
@@ -256,13 +270,14 @@
     def stage4(l):
         wgrad[l] = w3r[l].reshape(C, H).astype(F32)
 
-    moving = rims(u0p, 0)
+    moving = lat_rims(u0p, 0) + lon_rims(u0p, 0)
     for r in range(R):
         in_copies[R + r].wait()
         g1[r] = regroup(cotraw, r)
     finish(moving)
 
-    def block0(r):
+    def block0(i):
+        r = inward(i)
         conv_norm(u0p, 0, r, hid0, rc0, r)
         d0[r] = mix(hid0[r], 0)
 
@@ -274,8 +289,10 @@
 
         chunks(go)
 
-    rows_loop(0, R, block0)
-    moving = rims(u1p, 1)
+    rows_loop(0, 1, block0)
+    moving = lat_rims(u1p, 1)
+    rows_loop(1, R, block0)
+    moving += lon_rims(u1p, 1)
 
     def slopes(r):
         def go(a):
@@ -287,7 +304,8 @@
     rows_loop(0, R, slopes)
     finish(moving)
 
-    def block1(r):
+    def block1(i):
+        r = inward(i)
         conv_norm(u1p, 1, r, hid1, rc1, 0)
         pre[...] = mix(hid1[r], 1)
 
@@ -300,13 +318,16 @@
         pre[...] = mix_back(gp[r], 1)
         norm_back(g1p, hid1, rc1, r, 0)
 
-    rows_loop(0, R, block1)
-    moving = rims(g1p, 2)
+    rows_loop(0, 1, block1)
+    moving = lat_rims(g1p, 2)
+    rows_loop(1, R, block1)
+    moving += lon_rims(g1p, 2)
     weight_sum(1, hid1)
     sums = stage0(1)
     finish(moving)
 
-    def back0(r):
+    def back0(i):
+        r = inward(i)
         def go(a):
             for lanes in groups:
                 s = wide(g1[r, pl.ds(a, ch), :, lanes])
@@ -323,11 +344,13 @@
         norm_back(g0p, hid0, rc0, r, r)
 
     cuts = [(R * i) // 3 for i in range(4)]
+    rows_loop(0, 1, back0)
+    moving = lat_rims(g0p, 3)
     for i, stage in enumerate((stage1, stage2, stage3)):
-        rows_loop(cuts[i], cuts[i + 1], back0)
+        rows_loop(max(cuts[i], 1), cuts[i + 1], back0)
         finish(sums)
         sums = stage(1)
-    moving = rims(g0p, 3)
+    moving += lon_rims(g0p, 3)
     weight_sum(0, hid0)
     finish(sums)
     sums = stage0(0)

time: 124 us -> 120 us (0.968)
  Pallas kernels: 116 us -> 112 us
    pallas_call x1, Pallas kernels: 116 us -> 112 us  [body(): pl.pallas_call(functools.partial(kernel, n, 1.0 / math.sqrt(samples)), ou...]
where the time goes in v2:
time: 120 us
  Pallas kernels  112 us (93%)
  local copies, waits for them, and re-layouts  7.29 us (6%)
    pallas_call x1, Pallas kernels, body(): pl.pallas_call(functools.partial(kernel, n, 1.0 / math.sqrt(samples)), ou...  112 us
    unnamed x5, local copies, waits for them, and re-layouts  5.91 us

profile of v2, /device:TPU:0, one launch (start us, length us, event | category | flops | bytes accessed | tf_op | source)
XLA Modules:
  0.0 120.1 jit_solution(10159285670053726211)
XLA Ops:
  0.6 1.3 %copy.7.dw_ref = bf16[2,9,512]{2,1,0:T(8,128)(2,1)} copy(bf16[2,9,512]{2,0,1:T(2,128)(2,1)} %param.6) | data formatting | bytes 36864 | tf_op args[2]
  2.0 112.2 %blocks.1 = (bf16[1,24,112,512]{3,2,1,0:T(8,128)(2,1)}, f32[2,9,256]{2,1,0:T(8,128)}, f32[2,512,256]{2,1,0:T(8,128)}) custom-call(bf16[1,24,112,512]{3,2,1,0:T(8,128)(2,1)} %x_hbm.1, bf16[1,24,112,512]{3,2,1,0:T(8,128)(2,1)} %cot_hbm.1, bf16[2,9,512]{2,1,0:T(8,128)(2,1)} %copy.7.dw_ref, bf16[2,512,512]{2,1,0:T(8,128)(2,1)} %w_ref.1), custom_call_target="tpu_custom_call" | custom-call | tf_op jit(solution)/shard_map/blocks/pallas_call | solution.py:438
  114.1 1.4 %copy.8 = f32[2,9,256]{2,0,1:T(2,128)} copy(f32[2,9,256]{2,1,0:T(8,128)} %get-tuple-element.4) | data formatting | bytes 36864 | tf_op jit(solution)/shard_map/blocks/pallas_call | solution.py:438
  115.5 0.0 copy-start
  115.5 3.6 %copy.11 = bf16[1,24,112,512]{3,2,1,0:T(8,128)(2,1)} copy(bf16[1,24,112,512]{3,2,1,0:T(8,128)(2,1)} %get-tuple-element.9) | data formatting | bytes 5505024
  119.1 0.0 copy-done
  119.1 1.0 copy.12
Async XLA Ops:
  115.5 3.6 %copy-start = (f32[2,512,256]{2,1,0:T(8,128)S(1)}, f32[2,512,256]{2,1,0:T(8,128)}, u32[]{:S(2)}) copy-start(f32[2,512,256]{2,1,0:T(8,128)} %get-tuple-element.11) | copy-start | bytes 3145732
